TPU v7x, 256 devices: a whole 4x4x8 slice. The times are simulated.
256 devices in a mesh: leaf: 4 (over x), dof: 4 (over y), blk: 16 (over z, core).
Axes of the slice: x: 4, y: 4, z: 8, core: 2. Of those that a mesh axis runs over, the one named last changes fastest.
Arguments:
- modes: bfloat16 [4, 128, 128, 16, 128], P('leaf', 'blk', 'dof'), may hold values from -1.5 to 1.5
- stiffness: float32 [4, 128, 16, 128], P('leaf', 'dof'), may hold values from 0.25 to 2
- density: float32 [4, 128, 16, 128], P('leaf', 'dof'), may hold values from 0.5 to 4
- eigen_blocks: bfloat16 [4, 128, 128], P('leaf', None, 'blk'), may hold values from -0.5 to 0.5
- parent: int32 [4], replicated, may hold values from 0 to 1
Outputs:
- node_stiffness: float32 [2, 128, 128], P(None, 'blk')
- root_stiffness: float32 [128, 128], P('blk')
- leaf_vectors: bfloat16 [4, 128, 128, 16, 128], P('leaf', 'blk', 'dof')
All inputs are finite; a program needn't handle non-finite values.
Results may differ from a plain program's by a relative error of at most 0.0035.
Values may be sent and summed in bfloat16 or wider, within the bound.
A program may use at most 64 MiB of HBM per device.

v0:
```python
import functools

import jax
import jax.numpy as jnp
from jax import lax
from jax.sharding import PartitionSpec as P


def extended(x, sides, width):
    for axis, dim in sides:
        size, length = (lax.axis_size(axis), x.shape[dim])
        up = [(i, (i + 1) % size) for i in range(size - 1)]
        down = [(j, i) for i, j in up]
        last = lax.slice_in_dim(x, length - width, length, axis=dim)
        leading = lax.slice_in_dim(x, 0, width, axis=dim)
        before = lax.ppermute(last, axis, up)
        after = lax.ppermute(leading, axis, down)
        x = jnp.concatenate([before, x, after], axis=dim)
    return x


def copy_for_each(x, axis):
    length = lax.axis_size(axis)
    return lax.all_to_all(jnp.broadcast_to(x[None], (length, *x.shape)), axis, 0, 0, tiled=True)


def joined_along(parts, dim):
    parts = jnp.moveaxis(parts, 0, dim)
    shape = parts.shape
    return parts.reshape(*shape[:dim], shape[dim] * shape[dim + 1], *shape[dim + 2 :])


def gather_directly(x, axis, dim):
    parts = copy_for_each(x, axis)
    return joined_along(parts, dim)


def split_up(x, dim, length):
    before, after = (x.shape[:dim], x.shape[dim + 1 :])
    return jnp.moveaxis(x.reshape(*before, length, -1, *after), dim, 0)


def summed_on_arrival(x, axis, dim):
    length = lax.axis_size(axis)
    parts = lax.all_to_all(split_up(x, dim, length), axis, 0, 0, tiled=True)
    return jnp.sum(parts.astype(jnp.float32), axis=0)


def by_axis(x, axes):
    return functools.reduce(lax.psum, axes, x)


def neighbours(padded):
    inner = padded[:, 1:-1]
    sides = jnp.pad(inner, ((0, 0), (0, 0), (1, 1), (1, 1)))
    total = padded[:, 2:] + padded[:, :-2]
    total = total + sides[:, :, 2:, 1:-1] + sides[:, :, :-2, 1:-1]
    total = total + sides[:, :, 1:-1, 2:] + sides[:, :, 1:-1, :-2]
    return total


def body(modes, stiffness, density, eigen_blocks, parent):
    own = modes[0]
    rows, cells_x, cells_y, cells_z = own.shape
    cells = cells_x * cells_y * cells_z
    padded = extended(own, (("dof", 1),), 1).astype(jnp.float32)
    field = padded[:, 1:-1]
    stiff = ((6.0 + stiffness[0]) * field - neighbours(padded)).astype(jnp.bfloat16)
    stiff_flat = stiff.reshape(rows, cells)
    own_flat = own.reshape(rows, cells)
    mass_flat = density[0].reshape(cells)
    weighed_own = (mass_flat[None, :] * own_flat.astype(jnp.float32)).astype(jnp.bfloat16)
    diag_own = jnp.einsum("rc,rc->r", weighed_own, own_flat, preferred_element_type=jnp.float32)
    diagonal = gather_directly(diag_own, "blk", 0)
    blocks = eigen_blocks[0]
    eig_rows = blocks.shape[1]
    mode_cells, stiff_cells = (
        lax.all_to_all(own_flat, "blk", split_axis=1, concat_axis=0, tiled=True),
        lax.all_to_all(stiff_flat, "blk", split_axis=1, concat_axis=0, tiled=True),
    )
    partial_value = lax.dot_general(
        stiff_cells, mode_cells, (((1,), (1,)), ((), ())), preferred_element_type=jnp.float32
    )
    reduced = summed_on_arrival(partial_value.astype(jnp.bfloat16), "blk", 0)
    all_blocks = lax.all_gather(blocks, "blk", axis=1, tiled=True)
    local_vectors = lax.dot_general(
        all_blocks, mode_cells, (((0,), (0,)), ((), ())), preferred_element_type=jnp.float32
    ).astype(jnp.bfloat16)
    vector_flat = lax.all_to_all(local_vectors, "blk", split_axis=0, concat_axis=1, tiled=True)
    leaf_vectors = vector_flat.reshape(1, eig_rows, cells_x, cells_y, cells_z)
    leaves = lax.axis_size("leaf")
    nodes = leaves // 2
    node_ids = jnp.arange(nodes, dtype=jnp.int32)
    leaf_id = lax.axis_index("leaf")
    my_parent = jnp.sum(jnp.where(jnp.arange(leaves, dtype=jnp.int32) == leaf_id, parent, 0))
    slot = (node_ids == my_parent).astype(jnp.float32)
    node_stiffness, node_mass = (
        by_axis(slot[:, None, None] * reduced[None], ("leaf", "dof")),
        by_axis(slot[:, None] * diagonal[None], ("leaf", "dof")),
    )
    scale = 1.0 / jnp.sqrt(node_mass)
    scale_own = lax.dynamic_slice_in_dim(scale, lax.axis_index("blk") * rows, rows, 1)
    root_stiffness = jnp.sum(scale_own[:, :, None] * node_stiffness * scale[:, None, :], axis=0)
    return (node_stiffness, root_stiffness, leaf_vectors)


def solution(mesh):
    in_specs = (
        P("leaf", "blk", "dof", None, None),
        P("leaf", "dof", None, None),
        P("leaf", "dof", None, None),
        P("leaf", None, "blk"),
        P(),
    )
    out_specs = (P(None, "blk", None), P("blk", None), P("leaf", "blk", "dof", None, None))
    return jax.shard_map(body, mesh=mesh, in_specs=in_specs, out_specs=out_specs, check_vma=False)
```

profile of v0, /device:TPU:1, one launch (start us, length us, event | category | flops | bytes accessed | tf_op | source)
XLA Modules:
  0.0 142.7 jit_solution(9911222080380538267)
XLA Ops:
  0.6 1.5 %all_to_all.51 = bf16[8,16,4096]{2,1,0:T(8,128)(2,1)S(1)} reshape(bf16[1,8,32,16,128]{4,3,2,1,0:T(8,128)(2,1)} %param.5) | data formatting | bytes 2097152 | tf_op jit(solution)/shard_map/all_to_all | solution.py:78
  2.2 1.6 %copy.14 = bf16[8,16,4096]{2,0,1:T(8,128)(2,1)} copy(bf16[8,16,4096]{2,1,0:T(8,128)(2,1)S(1)} %all_to_all.51) | data formatting | bytes 2097152 | tf_op jit(solution)/shard_map/all_to_all | solution.py:78
  3.8 10.0 %all-to-all-start.1 = ((bf16[8,16,4096]{2,0,1:T(8,128)(2,1)}), bf16[8,16,4096]{2,0,1:T(8,128)(2,1)S(1)}, u32[]{:S(2)}, u32[]{:S(2)}) async-start(bf16[8,16,4096]{2,0,1:T(8,128)(2,1)} %copy.14), calls=%async_computation.1 | async-start | bytes 2097152 | tf_op jit(solution)/shard_map/all_to_all | solution.py:78
  13.7 3.2 %collective-permute-start = (bf16[8,1,16,128]{3,2,1,0:T(8,128)(2,1)S(1)}, bf16[8,1,16,128]{3,2,1,0:T(8,128)(2,1)S(1)}, u32[]{:S(2)}, u32[]{:S(2)}) collective-permute-start(bf16[8,1,16,128]{3,2,1,0:T(8,128)(2,1)S(1)} %get-tuple-element.7), channel_id=1, source_target_pairs={{0,16},{16,32},{32,48},{1,17},{17,33},{33,49},{2,18},{18,34},{34,5... | collective-permute-start | bytes 98312 | tf_op jit(solution)/shard_map/ppermute | solution.py:16
  17.0 1.3 collective-permute-start.1
  18.3 3.6 %collective-permute-done.1 = bf16[8,1,16,128]{3,2,1,0:T(8,128)(2,1)S(1)} collective-permute-done((bf16[8,1,16,128]{3,2,1,0:T(8,128)(2,1)S(1)}, bf16[8,1,16,128]{3,2,1,0:T(8,128)(2,1)S(1)}, u32[]{:S(2)}, u32[]{:S(2)}) %collective-permute-start.1) | collective-permute-done | bytes 32800 | tf_op jit(solution)/shard_map/ppermute | solution.py:17
  22.3 2.1 %fusion.8 = bf16[8,32,16,128]{3,2,1,0:T(8,128)(2,1)} fusion(f32[8,32,16,128]{3,2,1,0:T(8,128)S(1)} %slice.39, f32[8,34,16,128]{3,2,1,0:T(8,128)S(1)} %maximum_convert_fusion, f32[32,16,128]{2,1,0:T(8,128)S(1)} %add_bitcast_fusion), kind=kLoop, calls=%fused_computation.15 | loop fusion | flops 4194304 | bytes 7602176 | tf_op jit(solution)/shard_map/convert_element_type | solution.py:68
  24.4 1.5 %all_to_all.47 = bf16[8,16,4096]{2,1,0:T(8,128)(2,1)S(1)} reshape(bf16[8,32,16,128]{3,2,1,0:T(8,128)(2,1)} %fusion.8) | data formatting | bytes 2097152 | tf_op jit(solution)/shard_map/all_to_all | solution.py:79
  25.9 1.6 %copy.13 = bf16[8,16,4096]{2,0,1:T(8,128)(2,1)} copy(bf16[8,16,4096]{2,1,0:T(8,128)(2,1)S(1)} %all_to_all.47) | data formatting | bytes 2097152 | tf_op jit(solution)/shard_map/all_to_all | solution.py:79
  27.5 14.2 %all-to-all-done.1 = bf16[8,16,4096]{2,0,1:T(8,128)(2,1)S(1)} async-done(((bf16[8,16,4096]{2,0,1:T(8,128)(2,1)}), bf16[8,16,4096]{2,0,1:T(8,128)(2,1)S(1)}, u32[]{:S(2)}, u32[]{:S(2)}) %all-to-all-start.1) | async-done | bytes 1048608 | tf_op jit(solution)/shard_map/all_to_all | solution.py:78
  41.7 3.6 %all-to-all-start = ((bf16[8,16,4096]{2,0,1:T(8,128)(2,1)}), bf16[8,16,4096]{2,0,1:T(8,128)(2,1)S(1)}, u32[]{:S(2)}, u32[]{:S(2)}) async-start(bf16[8,16,4096]{2,0,1:T(8,128)(2,1)} %copy.13), calls=%async_computation | async-start | bytes 2097152 | tf_op jit(solution)/shard_map/all_to_all | solution.py:79
  45.3 1.4 %reshape_squeeze.3 = bf16[8,65536]{1,0:T(8,128)(2,1)} reshape(bf16[1,8,32,16,128]{4,3,2,1,0:T(8,128)(2,1)S(1)} %copy-done) | data formatting | bytes 2097152 | tf_op jit(solution)/shard_map/reshape;squeeze | solution.py:70
  46.7 35.2 %all-gather = bf16[1,128,128]{1,2,0:T(8,128)(2,1)S(1)} all-gather(bf16[1,128,8]{1,2,0:T(8,128)(2,1)S(1)} %copy-done.4), channel_id=2, replica_groups=mesh['leaf'=4,'dof'=4,'blk'=16] {'blk'}, dimensions={2}, use_global_device_ids=true | all-gather | bytes 34816 | tf_op jit(solution)/shard_map/all_gather | solution.py:85
  81.9 1.9 %fusion.2 = f32[8]{0:T(128)S(1)} fusion(bf16[8,65536]{1,0:T(8,128)(2,1)} %reshape_squeeze.3, f32[65536]{0:T(1024)S(1)} %bitcast.33), kind=kLoop, calls=%fused_computation.9 | loop fusion | flops 3145720 | bytes 1310752 | tf_op jit(solution)/shard_map/rc,rc->r/dot_general | solution.py:73
  83.8 0.6 broadcast_in_dim.7
  84.4 6.1 %all-to-all-start.3 = ((f32[16,1,8]{2,1,0:T(1,128)}), f32[16,1,8]{2,1,0:T(1,128)S(1)}, u32[]{:S(2)}, u32[]{:S(2)}) async-start(f32[16,1,8]{2,1,0:T(1,128)} %broadcast_in_dim.7), calls=%async_computation.3 | async-start | bytes 16384 | tf_op jit(solution)/shard_map/all_to_all | solution.py:24
  90.5 1.1 fusion.9
  91.6 5.9 %all-to-all-done.3 = f32[16,1,8]{2,1,0:T(1,128)S(1)} async-done(((f32[16,1,8]{2,1,0:T(1,128)}), f32[16,1,8]{2,1,0:T(1,128)S(1)}, u32[]{:S(2)}, u32[]{:S(2)}) %all-to-all-start.3) | async-done | bytes 544 | tf_op jit(solution)/shard_map/all_to_all | solution.py:24
  97.5 3.9 %all-to-all-start.2 = ((bf16[16,8,128]{2,1,0:T(8,128)(2,1)}), bf16[16,8,128]{2,1,0:T(8,128)(2,1)S(1)}, u32[]{:S(2)}, u32[]{:S(2)}) async-start(bf16[16,8,128]{2,1,0:T(8,128)(2,1)} %fusion.9), calls=%async_computation.2 | async-start | bytes 65536 | tf_op jit(solution)/shard_map/all_to_all | solution.py:45
  101.4 1.4 fusion
  102.8 6.1 %all-to-all-done.2 = bf16[16,8,128]{2,1,0:T(8,128)(2,1)S(1)} async-done(((bf16[16,8,128]{2,1,0:T(8,128)(2,1)}), bf16[16,8,128]{2,1,0:T(8,128)(2,1)S(1)}, u32[]{:S(2)}, u32[]{:S(2)}) %all-to-all-start.2) | async-done | bytes 32800 | tf_op jit(solution)/shard_map/all_to_all | solution.py:45
  108.9 3.8 %all-to-all-start.4 = ((bf16[16,8,4096]{2,1,0:T(8,128)(2,1)}), bf16[16,8,4096]{2,1,0:T(8,128)(2,1)S(1)}, u32[]{:S(2)}, u32[]{:S(2)}) async-start(bf16[16,8,4096]{2,1,0:T(8,128)(2,1)} %fusion), calls=%async_computation.4 | async-start | bytes 2097152 | tf_op jit(solution)/shard_map/all_to_all | solution.py:89
  112.8 0.6 fusion.14
  113.4 0.6 compare_convert_fusion
  114.0 0.5 broadcast.20
  114.6 0.7 reduce.5
  115.5 9.3 %all-reduce.2 = (f32[2,8,128]{2,1,0:T(8,128)S(1)}, f32[2,128]{1,0:T(2,128)S(1)}) all-reduce(f32[2,8,128]{2,1,0:T(8,128)S(1)} %broadcast_multiply_fusion, f32[2,128]{1,0:T(2,128)S(1)} %broadcast_multiply_fusion.1), channel_id=1, replica_groups=mesh['leaf'=4,'dof'=4,'blk'=16] {'leaf'}, use_global_device_ids=true, to_apply=%region_2.3 | all-reduce | flops 2304 | bytes 18432 | tf_op jit(solution)/shard_map/psum | solution.py:50
  124.8 9.4 %all-reduce.1 = (f32[2,8,128]{2,1,0:T(8,128)S(1)}, f32[2,128]{1,0:T(2,128)S(1)}) all-reduce(f32[2,8,128]{2,1,0:T(8,128)S(1)} %get-tuple-element.5, f32[2,128]{1,0:T(2,128)S(1)} %get-tuple-element.6), channel_id=1, replica_groups=mesh['leaf'=4,'dof'=4,'blk'=16] {'dof'}, use_global_device_ids=true, to_apply=%region_3.4 | all-reduce | flops 2304 | bytes 18432 | tf_op jit(solution)/shard_map/psum | solution.py:50
  134.3 0.7 multiply_reduce_fusion
  134.9 5.8 %all-to-all-done.4 = bf16[16,8,4096]{2,1,0:T(8,128)(2,1)S(1)} async-done(((bf16[16,8,4096]{2,1,0:T(8,128)(2,1)}), bf16[16,8,4096]{2,1,0:T(8,128)(2,1)S(1)}, u32[]{:S(2)}, u32[]{:S(2)}) %all-to-all-start.4) | async-done | bytes 1048608 | tf_op jit(solution)/shard_map/all_to_all | solution.py:89
  140.8 0.6 copy.15
  141.4 1.3 reshape.48
  (24 shorter events, 0.8 us)
Async XLA Ops:
  2.2 11.6 %copy-start = (bf16[1,8,32,16,128]{4,3,2,1,0:T(8,128)(2,1)S(1)}, bf16[1,8,32,16,128]{4,3,2,1,0:T(8,128)(2,1)}, u32[]{:S(2)}) copy-start(bf16[1,8,32,16,128]{4,3,2,1,0:T(8,128)(2,1)} %param.5) | copy-start | bytes 3145732
  2.2 16.1 %copy-start.2 = (f32[1,32,16,128]{3,2,1,0:T(8,128)S(1)}, f32[1,32,16,128]{3,2,1,0:T(8,128)}, u32[]{:S(2)}) copy-start(f32[1,32,16,128]{3,2,1,0:T(8,128)} %param.6) | copy-start | bytes 786436
  3.8 38.0 %all-to-all-start.1 = ((bf16[8,16,4096]{2,0,1:T(8,128)(2,1)}), bf16[8,16,4096]{2,0,1:T(8,128)(2,1)S(1)}, u32[]{:S(2)}, u32[]{:S(2)}) async-start(bf16[8,16,4096]{2,0,1:T(8,128)(2,1)} %copy.14), calls=%async_computation.1 | async-start | bytes 2097152 | tf_op jit(solution)/shard_map/all_to_all | solution.py:78
  13.7 4.6 %collective-permute-start = (bf16[8,1,16,128]{3,2,1,0:T(8,128)(2,1)S(1)}, bf16[8,1,16,128]{3,2,1,0:T(8,128)(2,1)S(1)}, u32[]{:S(2)}, u32[]{:S(2)}) collective-permute-start(bf16[8,1,16,128]{3,2,1,0:T(8,128)(2,1)S(1)} %get-tuple-element.7), channel_id=1, source_target_pairs={{0,16},{16,32},{32,48},{1,17},{17,33},{33,49},{2,18},{18,34},{34,5... | collective-permute-start | bytes 98312 | tf_op jit(solution)/shard_map/ppermute | solution.py:16
  17.0 5.0 %collective-permute-start.1 = (bf16[8,1,16,128]{3,2,1,0:T(8,128)(2,1)S(1)}, bf16[8,1,16,128]{3,2,1,0:T(8,128)(2,1)S(1)}, u32[]{:S(2)}, u32[]{:S(2)}) collective-permute-start(bf16[8,1,16,128]{3,2,1,0:T(8,128)(2,1)S(1)} %get-tuple-element.8), channel_id=1, source_target_pairs={{16,0},{32,16},{48,32},{17,1},{33,17},{49,33},{18,2},{34,18},{50,3... | collective-permute-start | bytes 98312 | tf_op jit(solution)/shard_map/ppermute | solution.py:17
  27.5 19.2 %copy-start.4 = (bf16[1,128,8]{1,2,0:T(8,128)(2,1)S(1)}, bf16[1,128,8]{1,2,0:T(8,128)(2,1)}, u32[]{:S(2)}) copy-start(bf16[1,128,8]{1,2,0:T(8,128)(2,1)} %param.8) | copy-start | bytes 6148
  27.5 54.4 %copy-start.1 = (f32[1,32,16,128]{3,2,1,0:T(8,128)S(1)}, f32[1,32,16,128]{3,2,1,0:T(8,128)}, u32[]{:S(2)}) copy-start(f32[1,32,16,128]{3,2,1,0:T(8,128)} %param.7) | copy-start | bytes 786436
  41.7 42.1 %all-to-all-start = ((bf16[8,16,4096]{2,0,1:T(8,128)(2,1)}), bf16[8,16,4096]{2,0,1:T(8,128)(2,1)S(1)}, u32[]{:S(2)}, u32[]{:S(2)}) async-start(bf16[8,16,4096]{2,0,1:T(8,128)(2,1)} %copy.13), calls=%async_computation | async-start | bytes 2097152 | tf_op jit(solution)/shard_map/all_to_all | solution.py:79
  84.4 13.1 %all-to-all-start.3 = ((f32[16,1,8]{2,1,0:T(1,128)}), f32[16,1,8]{2,1,0:T(1,128)S(1)}, u32[]{:S(2)}, u32[]{:S(2)}) async-start(f32[16,1,8]{2,1,0:T(1,128)} %broadcast_in_dim.7), calls=%async_computation.3 | async-start | bytes 16384 | tf_op jit(solution)/shard_map/all_to_all | solution.py:24
  97.5 11.4 %all-to-all-start.2 = ((bf16[16,8,128]{2,1,0:T(8,128)(2,1)}), bf16[16,8,128]{2,1,0:T(8,128)(2,1)S(1)}, u32[]{:S(2)}, u32[]{:S(2)}) async-start(bf16[16,8,128]{2,1,0:T(8,128)(2,1)} %fusion.9), calls=%async_computation.2 | async-start | bytes 65536 | tf_op jit(solution)/shard_map/all_to_all | solution.py:45
  101.4 11.3 %copy-start.5 = (s32[4]{0:T(128)S(1)}, s32[4]{0:T(128)}, u32[]{:S(2)}) copy-start(s32[4]{0:T(128)} %param.9) | copy-start | bytes 52
  108.9 31.9 %all-to-all-start.4 = ((bf16[16,8,4096]{2,1,0:T(8,128)(2,1)}), bf16[16,8,4096]{2,1,0:T(8,128)(2,1)S(1)}, u32[]{:S(2)}, u32[]{:S(2)}) async-start(bf16[16,8,4096]{2,1,0:T(8,128)(2,1)} %fusion), calls=%async_computation.4 | async-start | bytes 2097152 | tf_op jit(solution)/shard_map/all_to_all | solution.py:89
  134.2 8.5 %copy-start.3 = (f32[2,8,128]{2,1,0:T(8,128)}, f32[2,8,128]{2,1,0:T(8,128)S(1)}, u32[]{:S(2)}) copy-start(f32[2,8,128]{2,1,0:T(8,128)S(1)} %get-tuple-element.3) | copy-start | bytes 24580
where the time goes:
time: 143 us
  blocking collectives  53.9 us (38%)
  waiting for transfers between devices  35.7 us (25%)
  starting transfers between devices  31.9 us (22%)
  local copies, waits for them, and re-layouts  11 us (8%)
  other arithmetic  6.97 us (5%)
  matrix products  2.45 us (2%)
    all_gather x1, blocking collectives, body(): all_blocks = lax.all_gather(blocks, 'blk', axis=1, tiled=True)  35.2 us
    psum x2, blocking collectives, by_axis(): return functools.reduce(lax.psum, axes, x)  18.7 us
    all_to_all x1, waiting for transfers between devices, body(): lax.all_to_all(own_flat, 'blk', split_axis=1, concat_axis=0, tiled=True)  14.2 us
    all_to_all x1, starting transfers between devices, body(): lax.all_to_all(own_flat, 'blk', split_axis=1, concat_axis=0, tiled=True)  9.97 us
    all_to_all x1, starting transfers between devices, copy_for_each(): lax.all_to_all(jnp.broadcast_to(x[None], (length, *x.shape)), axis, 0, 0,...  6.14 us
    all_to_all x1, waiting for transfers between devices, summed_on_arrival(): parts = lax.all_to_all(split_up(x, dim, length), axis, 0, 0, tiled=True)  6.08 us
    all_to_all x1, waiting for transfers between devices, copy_for_each(): lax.all_to_all(jnp.broadcast_to(x[None], (length, *x.shape)), axis, 0, 0,...  5.91 us
    all_to_all x1, waiting for transfers between devices, body(): lax.all_to_all(local_vectors, 'blk', split_axis=0, concat_axis=1, tiled=T...  5.84 us
  transfers between devices with their start and end apart: 7, of which 5 were waited for; matrix products, arithmetic and copies ran while one was open for 9% of the time, Pallas kernels for 0%

commit v1 on v0

v1 whole, which is shorter than its diff:
```python
import jax
import jax.numpy as jnp
from jax import lax
from jax.experimental import pallas as pl
from jax.experimental.pallas import tpu as pltpu
from jax.sharding import PartitionSpec as P

MESH = pl.DeviceIdType.MESH
F32 = jnp.float32
BF16 = jnp.bfloat16


def ring_order(chips):
    half = chips // 2
    steps = [half] + [s for d in range(half - 1, 0, -1) for s in (d, chips - d)]
    return [(dz, dc) for dz in steps for dc in (0, 1)] + [(0, 1)]


def kernel(
    sizes,
    modes,
    stiffness,
    density,
    eigen,
    parent,
    node_out,
    root_out,
    vec_out,
    own,
    dens,
    coef,
    eig_in,
    eig_send,
    eig,
    land,
    wide,
    phi,
    lhs,
    tall,
    vecs,
    edge,
    kfull,
    ksend,
    kland,
    msend,
    mland,
    psend,
    pland,
    load_sem,
    in_send,
    in_recv,
    e_send,
    e_recv,
    out_send,
    out_recv,
    k_send,
    k_recv,
    m_send,
    m_recv,
    p_send,
    p_recv,
    h_send,
    h_recv,
):
    leaves, dofs, blks = sizes
    chips = blks // 2
    rows, layers, cy, cz = own.shape
    n_modes = rows * blks
    half = cy // 2
    x, y, b = lax.axis_index("leaf"), lax.axis_index("dof"), lax.axis_index("blk")
    z, c = b // 2, lax.rem(b, 2)

    def layer_of(zz, cc, h):
        return 4 * zz + (3 * cc if h == 0 else 1 + cc)

    def column_peer(dz, dc):
        zz = lax.rem(z + dz, chips)
        cc = lax.rem(c + dc, 2)
        return zz, cc, zz * 2 + cc

    peers = [column_peer(dz, dc) for dz, dc in ring_order(chips)]
    plane = [(i, j) for i in range(leaves) for j in range(dofs) if (i, j) != (0, 0)]
    plane = [(lax.rem(x + i, leaves), lax.rem(y + j, dofs)) for i, j in plane]

    step = 2 * c - 1
    pz_raw = z + step
    pz = lax.rem(pz_raw + chips, chips)
    wraps = jnp.where(c == 1, jnp.where(z == chips - 1, 1, 0), jnp.where(z == 0, 1, 0))
    py = lax.rem(y + step * wraps + dofs, dofs)
    pb = pz * 2 + (1 - c)
    at_end = jnp.where(c == 1, jnp.where(y == dofs - 1, 1, 0), jnp.where(y == 0, 1, 0)) * wraps
    edge_weight = jnp.where(at_end == 1, 0.0, -2.0).astype(F32)

    loads = [
        pltpu.make_async_copy(eigen.at[0], eig_in, load_sem.at[0]),
        pltpu.make_async_copy(modes.at[0], own, load_sem.at[1]),
        pltpu.make_async_copy(density.at[0], dens, load_sem.at[2]),
        pltpu.make_async_copy(stiffness.at[0, pl.ds(layer_of(z, c, 0), 1)], coef.at[pl.ds(0, 1)], load_sem.at[3]),
        pltpu.make_async_copy(stiffness.at[0, pl.ds(layer_of(z, c, 1), 1)], coef.at[pl.ds(1, 1)], load_sem.at[4]),
    ]
    for cp in loads:
        cp.start()

    barrier = pltpu.get_barrier_semaphore()
    for _, _, p in peers:
        pl.semaphore_signal(barrier, inc=1, device_id={"blk": p}, device_id_type=MESH)
    for i, j in plane:
        pl.semaphore_signal(barrier, inc=1, device_id={"leaf": i, "dof": j}, device_id_type=MESH)
    pl.semaphore_signal(barrier, inc=1, device_id={"dof": py, "blk": pb}, device_id_type=MESH)

    loads[0].wait()
    eig_t = eig_in[...].astype(F32).T
    eig_send[...] = eig_t
    my_rows = pl.ds(pl.multiple_of(b * rows, rows), rows)
    eig[my_rows, :] = eig_t

    pl.semaphore_wait(barrier, len(peers) + len(plane) + 1)

    e_copies = []
    in_copies = [[], []]
    for n, (zz, cc, p) in enumerate(peers):
        cp = pltpu.make_async_remote_copy(
            eig_send, eig.at[my_rows], e_send.at[n], e_recv.at[n], device_id={"blk": p}, device_id_type=MESH
        )
        cp.start()
        e_copies.append(cp)
    for h in range(2):
        for n, (zz, cc, p) in enumerate(peers):
            cp = pltpu.make_async_remote_copy(
                modes.at[0, :, layer_of(zz, cc, h)],
                land.at[h, my_rows],
                in_send.at[h, n],
                in_recv.at[h, n],
                device_id={"blk": p},
                device_id_type=MESH,
            )
            cp.start()
            in_copies[h].append(cp)
    local_in = [
        pltpu.make_async_copy(modes.at[0, :, layer_of(z, c, h)], land.at[h, my_rows], load_sem.at[5 + h])
        for h in range(2)
    ]
    for cp in local_in:
        cp.start()

    loads[1].wait()
    loads[2].wait()

    def mass_step(i, acc):
        f = own[:, i].astype(F32)
        w = (dens[i][None] * f).astype(BF16).astype(F32)
        return acc + w * f

    acc = lax.fori_loop(0, layers, mass_step, jnp.zeros((rows, cy, cz), F32))
    mass = jnp.sum(jnp.sum(acc, axis=1), axis=1, keepdims=True)
    lane = lax.broadcasted_iota(jnp.int32, (rows, n_modes), 1)
    sub = lax.broadcasted_iota(jnp.int32, (rows, n_modes), 0)
    mine = lane == sub + b * rows
    mass_row = jnp.sum(jnp.where(mine, mass, 0.0), axis=0, keepdims=True)
    msend[...] = mass_row
    m_copies = []
    for n, (_, _, p) in enumerate(peers):
        cp = pltpu.make_async_remote_copy(
            msend, mland.at[n], m_send.at[n], m_recv.at[n], device_id={"blk": p}, device_id_type=MESH
        )
        cp.start()
        m_copies.append(cp)
    loads[3].wait()
    loads[4].wait()

    last_lane = lax.broadcasted_iota(jnp.int32, (n_modes, cz), 1) == cz - 1

    def relayout(h):
        wide[...] = land[h].reshape(n_modes * cy, cz).astype(F32)
        for j in range(cy):
            phi[h, :, j * cz : (j + 1) * cz] = wide[pl.ds(j, n_modes, stride=cy), :].astype(BF16)

    def send_edge(h, device):
        cp = pltpu.make_async_remote_copy(
            phi.at[h, :, pl.ds(pl.multiple_of(c * half * cz, half * cz), half * cz)],
            edge.at[h],
            h_send.at[h],
            h_recv.at[h],
            device_id=device,
            device_id_type=MESH,
        )
        cp.start()
        return cp

    def expand(h):
        e = eig[...].astype(BF16)
        for j in range(0, cy, 2):
            v = jnp.dot(e, phi[h, :, j * cz : (j + 2) * cz], preferred_element_type=F32)
            tall[pl.ds(j, n_modes, stride=cy), :] = v[:, :cz]
            tall[pl.ds(j + 1, n_modes, stride=cy), :] = v[:, cz:]
        vecs[h] = tall[...].astype(BF16).reshape(n_modes, cy, cz)

    def send_vectors(h):
        cps = []
        for n, (_, _, p) in enumerate(peers):
            cp = pltpu.make_async_remote_copy(
                vecs.at[h, pl.ds(pl.multiple_of(p * rows, rows), rows)],
                vec_out.at[:, layer_of(z, c, h)],
                out_send.at[h, n],
                out_recv.at[h, n],
                device_id={"blk": p},
                device_id_type=MESH,
            )
            cp.start()
            cps.append(cp)
        cp = pltpu.make_async_copy(vecs.at[h, my_rows], vec_out.at[:, layer_of(z, c, h)], load_sem.at[7 + h])
        cp.start()
        return cps, cp

    def images(h, other):
        nxt = wide[pl.ds(0, n_modes, stride=cy), :]
        for j in range(cy):
            f = nxt
            s = coef[h, j : j + 1, :] + 6.0
            side = jnp.where(last_lane, 0.0, pltpu.roll(f, cz - 1, 1))
            if j + 1 < cy:
                nxt = wide[pl.ds(j + 1, n_modes, stride=cy), :]
                side = side + nxt
            if other is not None:
                side = side + phi[other, :, j * cz : (j + 1) * cz].astype(F32)
            lhs[:, j * cz : (j + 1) * cz] = (s * f - 2.0 * side).astype(BF16)
        return lax.dot_general(lhs[...], phi[h], (((1,), (1,)), ((), ())), preferred_element_type=F32)

    def edge_product(h):
        part = phi[h, :, pl.ds(pl.multiple_of((1 - c) * half * cz, half * cz), half * cz)]
        return lax.dot_general(edge[h], part, (((1,), (1,)), ((), ())), preferred_element_type=F32)

    for cp in in_copies[0]:
        cp.wait_recv()
    local_in[0].wait()
    relayout(0)
    edge0 = send_edge(0, {"dof": py, "blk": pb})
    for cp in e_copies:
        cp.wait_recv()
    expand(0)
    out0, local0 = send_vectors(0)
    kfull[...] = images(0, None)
    edge0.wait_recv()
    kfull[...] += edge_weight * edge_product(0)

    for cp in in_copies[1]:
        cp.wait_recv()
    local_in[1].wait()
    relayout(1)
    edge1 = send_edge(1, {"blk": z * 2 + (1 - c)})
    kfull[...] += images(1, 0)
    edge1.wait_recv()
    total = kfull[...] - 2.0 * edge_product(1)
    kfull[...] = 0.5 * (total + total.T)
    for i in range(blks):
        ksend[i] = kfull[i * rows : (i + 1) * rows, :].astype(BF16)
    k_copies = []
    for n, (_, _, p) in enumerate(peers):
        cp = pltpu.make_async_remote_copy(
            ksend.at[p], kland.at[n], k_send.at[n], k_recv.at[n], device_id={"blk": p}, device_id_type=MESH
        )
        cp.start()
        k_copies.append(cp)
    expand(1)
    out1, local1 = send_vectors(1)

    mass_total = mass_row
    for n, cp in enumerate(m_copies):
        cp.wait_recv()
        mass_total = mass_total + mland[n]
    k_total = ksend[b].astype(F32)
    for n, cp in enumerate(k_copies):
        cp.wait_recv()
        k_total = k_total + kland[n].astype(F32)
    psend[:rows] = k_total
    psend[rows:] = jnp.broadcast_to(mass_total, (rows, n_modes))
    p_copies = []
    slot = x * dofs + y
    for n, (i, j) in enumerate(plane):
        cp = pltpu.make_async_remote_copy(
            psend, pland.at[slot], p_send.at[n], p_recv.at[n], device_id={"leaf": i, "dof": j}, device_id_type=MESH
        )
        cp.start()
        p_copies.append(cp)
    pland[slot] = psend[...]
    for cp in p_copies:
        cp.wait_recv()
    per_leaf = []
    for i in range(leaves):
        t = pland[i * dofs]
        for j in range(1, dofs):
            t = t + pland[i * dofs + j]
        per_leaf.append(t)
    root = jnp.zeros((rows, n_modes), F32)
    for node in range(node_out.shape[0]):
        t = jnp.zeros((2 * rows, n_modes), F32)
        for i in range(leaves):
            t = t + jnp.where(parent[i] == node, 1.0, 0.0).astype(F32) * per_leaf[i]
        node_out[node] = t[:rows]
        scale = 1.0 / jnp.sqrt(t[rows:])
        scale_own = jnp.sum(jnp.where(mine, scale, 0.0), axis=1, keepdims=True)
        root = root + scale_own * t[:rows] * scale
    root_out[...] = root

    for cp in in_copies[0] + in_copies[1] + e_copies + m_copies + k_copies + p_copies + [edge0, edge1]:
        cp.wait_send()
    for cp in out0 + out1:
        cp.wait()
    local0.wait()
    local1.wait()


def solution(mesh):
    leaves, dofs, blks = (mesh.shape[a] for a in ("leaf", "dof", "blk"))

    def body(modes, stiffness, density, eigen_blocks, parent):
        _, rows, layers, cy, cz = modes.shape
        n_modes = rows * blks
        cells = cy * cz
        others = blks - 1
        planes = leaves * dofs - 1
        dma = pltpu.SemaphoreType.DMA
        any_spec = pl.BlockSpec(memory_space=pl.ANY)
        vmem_spec = pl.BlockSpec(memory_space=pltpu.VMEM)
        node, root, vectors = pl.pallas_call(
            lambda *refs: kernel((leaves, dofs, blks), *refs),
            out_shape=(
                jax.ShapeDtypeStruct((leaves // 2, rows, n_modes), F32),
                jax.ShapeDtypeStruct((rows, n_modes), F32),
                jax.ShapeDtypeStruct((rows, layers, cy, cz), BF16),
            ),
            in_specs=[any_spec] * 4 + [pl.BlockSpec(memory_space=pltpu.SMEM)],
            out_specs=(vmem_spec, vmem_spec, any_spec),
            scratch_shapes=[
                pltpu.VMEM((rows, layers, cy, cz), BF16),
                pltpu.VMEM((layers, cy, cz), F32),
                pltpu.VMEM((2, cy, cz), F32),
                pltpu.VMEM((n_modes, rows), BF16),
                pltpu.VMEM((rows, n_modes), F32),
                pltpu.VMEM((n_modes, n_modes), F32),
                pltpu.VMEM((2, n_modes, cy, cz), BF16),
                pltpu.VMEM((n_modes * cy, cz), F32),
                pltpu.VMEM((2, n_modes, cells), BF16),
                pltpu.VMEM((n_modes, cells), BF16),
                pltpu.VMEM((n_modes * cy, cz), F32),
                pltpu.VMEM((2, n_modes, cy, cz), BF16),
                pltpu.VMEM((2, n_modes, cells // 2), BF16),
                pltpu.VMEM((n_modes, n_modes), F32),
                pltpu.VMEM((blks, rows, n_modes), BF16),
                pltpu.VMEM((others, rows, n_modes), BF16),
                pltpu.VMEM((1, n_modes), F32),
                pltpu.VMEM((others, 1, n_modes), F32),
                pltpu.VMEM((2 * rows, n_modes), F32),
                pltpu.VMEM((leaves * dofs, 2 * rows, n_modes), F32),
                dma((9,)),
                dma((2, others)),
                dma((2, others)),
                dma((others,)),
                dma((others,)),
                dma((2, others)),
                dma((2, others)),
                dma((others,)),
                dma((others,)),
                dma((others,)),
                dma((others,)),
                dma((planes,)),
                dma((planes,)),
                dma((2,)),
                dma((2,)),
            ],
            compiler_params=pltpu.CompilerParams(collective_id=0, has_side_effects=True),
            name="tree",
        )(modes, stiffness, density, eigen_blocks, parent)
        return node, root, vectors[None]

    in_specs = (
        P("leaf", "blk", "dof", None, None),
        P("leaf", "dof", None, None),
        P("leaf", "dof", None, None),
        P("leaf", None, "blk"),
        P(),
    )
    out_specs = (P(None, "blk", None), P("blk", None), P("leaf", "blk", "dof", None, None))
    return jax.shard_map(body, mesh=mesh, in_specs=in_specs, out_specs=out_specs, check_vma=False)
```

time: 143 us -> 72.9 us (0.51)
  Pallas kernels: 0 us -> 66.4 us
  blocking collectives: 53.9 us -> 0 us
  waiting for transfers between devices: 35.7 us -> 0 us
  starting transfers between devices: 31.9 us -> 0 us
  other arithmetic: 6.97 us -> 0 us
  local copies, waits for them, and re-layouts: 11 us -> 5.67 us
  matrix products: 2.45 us -> 0 us
    pallas_call x0 -> x1, Pallas kernels: none -> 66.4 us  [body(): pl.pallas_call(lambda *refs: kernel((leaves, dofs, blks), *refs), out_sha...]
    all_gather x1 -> x0, blocking collectives: 35.2 us -> none  [body(): all_blocks = lax.all_gather(blocks, 'blk', axis=1, tiled=True)]
    all_to_all x5 -> x0, waiting for transfers between devices: 32.1 us -> none  [the longest x1 14.2 us: body(): lax.all_to_all(own_flat, 'blk', split_axis=1, concat_axis=0, tiled=True)]
    all_to_all x5 -> x0, starting transfers between devices: 27.4 us -> none  [the longest x1 9.97 us: body(): lax.all_to_all(own_flat, 'blk', split_axis=1, concat_axis=0, tiled=True)]
    psum x2 -> x0, blocking collectives: 18.7 us -> none  [by_axis(): return functools.reduce(lax.psum, axes, x)]
    all_to_all x6 -> x0, local copies, waits for them, and re-layouts: 7.25 us -> none  [the longest x2 3.09 us: body(): lax.all_to_all(own_flat, 'blk', split_axis=1, concat_axis=0, tiled=True)]
    unnamed x12 -> x6, local copies, waits for them, and re-layouts: 0.03 us -> 5.67 us
    ppermute x2 -> x0, starting transfers between devices: 4.49 us -> none  [the longest x1 3.2 us: extended(): before = lax.ppermute(last, axis, up)]
  transfers between devices with their start and end apart: 7 -> 0, of which waited for: 5 -> 0; matrix products, arithmetic and copies ran while one was open for 9% -> 0% of each run, Pallas kernels for 0% -> 0%
where the time goes in v1:
time: 72.9 us; the launch traced here: 72.7 us
  Pallas kernels  66.4 us (91%)
  local copies, waits for them, and re-layouts  5.67 us (8%)
    pallas_call x1, Pallas kernels, body(): pl.pallas_call(lambda *refs: kernel((leaves, dofs, blks), *refs), out_sha...  66.4 us
    unnamed x6, local copies, waits for them, and re-layouts  5.67 us

profile of v1, /device:TPU:1, one launch (start us, length us, event | category | flops | bytes accessed | tf_op | source)
XLA Modules:
  0.0 72.7 jit_solution(2725919505561654388)
XLA Ops:
  0.6 1.4 %copy.8.refs_3_ = bf16[1,128,8]{2,1,0:T(8,128)(2,1)} copy(bf16[1,128,8]{1,2,0:T(8,128)(2,1)} %param.8) | data formatting | bytes 4096 | tf_op args[3]
  2.0 66.4 %tree.1 = (f32[2,8,128]{2,1,0:T(8,128)}, f32[8,128]{1,0:T(8,128)}, bf16[8,32,16,128]{3,2,1,0:T(8,128)(2,1)}) custom-call(bf16[1,8,32,16,128]{4,3,2,1,0:T(8,128)(2,1)} %refs_0_.1, f32[1,32,16,128]{3,2,1,0:T(8,128)} %refs_1_.1, f32[1,32,16,128]{3,2,1,0:T(8,128)} %refs_2_.1, bf16[1,128,8]{2,1,0:T(8,128)(2,1)} %copy.8.refs_3_, s32[4]{0:T(128)} %refs_4_.1), custom_call_target="tpu_custom_call" | custom-call | tf_op jit(solution)/shard_map/tree/pallas_call | solution.py:325
  68.4 0.0 copy-start
  68.4 1.3 %copy.12 = f32[2,8,128]{2,1,0:T(8,128)} copy(f32[2,8,128]{2,1,0:T(8,128)} %get-tuple-element.12) | data formatting | bytes 16384
  69.7 0.0 copy-done
  69.7 0.6 copy.13
  70.3 2.4 %copy.14 = bf16[1,8,32,16,128]{4,3,2,1,0:T(8,128)(2,1)} copy(bf16[1,8,32,16,128]{4,3,2,1,0:T(8,128)(2,1)} %bitcast.1) | data formatting | bytes 2097152
Async XLA Ops:
  68.4 1.3 %copy-start = (f32[8,128]{1,0:T(8,128)S(1)}, f32[8,128]{1,0:T(8,128)}, u32[]{:S(2)}) copy-start(f32[8,128]{1,0:T(8,128)} %get-tuple-element.13) | copy-start | bytes 12292

commit v2 on v1

v2 whole, which is shorter than its diff:
```python
import jax
import jax.numpy as jnp
from jax import lax
from jax.experimental import pallas as pl
from jax.experimental.pallas import tpu as pltpu
from jax.sharding import PartitionSpec as P

MESH = pl.DeviceIdType.MESH
F32 = jnp.float32
BF16 = jnp.bfloat16
FIRST_PART = 8


def ring_peers(chips):
    found = {}
    for dz in range(chips):
        for dc in range(2):
            if dz or dc:
                found.setdefault(min(dz, chips - dz) + dc, []).append((dz, dc))
    return [found[d] for d in sorted(found)]


def drain(ref, sem):
    pltpu.make_async_copy(ref, ref, sem).wait()


def kernel(
    sizes,
    first_part,
    modes,
    stiffness,
    density,
    eigen,
    parent_in,
    node_out,
    root_out,
    vec_out,
    parent,
    node,
    root_sum,
    own,
    dens,
    coef,
    eig_in,
    eig,
    land,
    wide,
    phi,
    lhs,
    tall,
    vecs,
    edge,
    kfull,
    ksend,
    kland,
    msend,
    mland,
    psend,
    pland,
    load_sem,
    in_recv,
    out_recv,
    h_recv,
    small_recv,
    send_sem,
    near_sem,
    plane_sem,
):
    leaves, dofs, blks = sizes
    chips = blks // 2
    rows, layers, cy, cz = own.shape
    n_modes = rows * blks
    half = cy // 2
    x, y, b = lax.axis_index("leaf"), lax.axis_index("dof"), lax.axis_index("blk")
    z, c = b // 2, lax.rem(b, 2)
    e_recv, k_recv, m_recv, p_recv = (small_recv.at[i] for i in range(4))
    in_send, e_send, out_send, k_send, m_send, p_send, h0_send, h1_send = (send_sem.at[i] for i in range(8))
    my_rows = pl.ds(pl.multiple_of(b * rows, rows), rows)

    def layer_of(zz, cc, h):
        return 4 * zz + (3 * cc if h == 0 else 1 + cc)

    def column_peer(dz, dc):
        zz = lax.rem(z + dz, chips)
        cc = lax.rem(c + dc, 2)
        return zz, cc, zz * 2 + cc

    rings = [[column_peer(dz, dc) for dz, dc in ring] for ring in ring_peers(chips)]
    peers = [p for ring in rings for p in ring]
    plane = [(i, j) for i in range(leaves) for j in range(dofs) if (i, j) != (0, 0)]
    plane = [(lax.rem(x + i, leaves), lax.rem(y + j, dofs)) for i, j in plane]

    step = 2 * c - 1
    pz = lax.rem(z + step + chips, chips)
    wraps = jnp.where(c == 1, jnp.where(z == chips - 1, 1, 0), jnp.where(z == 0, 1, 0))
    py = lax.rem(y + step * wraps + dofs, dofs)
    pb = pz * 2 + (1 - c)
    at_end = jnp.where(c == 1, jnp.where(y == dofs - 1, 1, 0), jnp.where(y == 0, 1, 0)) * wraps
    edge_weight = jnp.where(at_end == 1, 0.0, -2.0).astype(F32)

    near = [{"blk": p} for _, _, p in rings[0]]
    beside = [
        {"leaf": lax.rem(x + 1, leaves)},
        {"leaf": lax.rem(x + leaves - 1, leaves)},
        {"dof": lax.rem(y + 1, dofs)},
        {"dof": lax.rem(y + dofs - 1, dofs)},
    ]

    def tell(sem, devices):
        for device in devices:
            pl.semaphore_signal(sem, inc=1, device_id=device, device_id_type=MESH)

    barrier = pltpu.get_barrier_semaphore()
    tell(barrier, near + beside)
    loads = [
        pltpu.make_async_copy(eigen.at[0], eig_in, load_sem.at[0]),
        pltpu.make_async_copy(modes.at[0], own, load_sem.at[1]),
        pltpu.make_async_copy(density.at[0], dens, load_sem.at[2]),
        pltpu.make_async_copy(parent_in, parent, load_sem.at[3]),
        pltpu.make_async_copy(stiffness.at[0, pl.ds(layer_of(z, c, 0), 1)], coef.at[pl.ds(0, 1)], load_sem.at[4]),
        pltpu.make_async_copy(stiffness.at[0, pl.ds(layer_of(z, c, 1), 1)], coef.at[pl.ds(1, 1)], load_sem.at[4]),
    ]
    for cp in loads:
        cp.start()

    def remote(src, dst, send, recv, device):
        pltpu.make_async_remote_copy(src, dst, send, recv, device_id=device, device_id_type=MESH).start()

    def send_modes(h, peer):
        zz, cc, p = peer
        remote(modes.at[0, :, layer_of(zz, cc, h)], land.at[h, my_rows], in_send, in_recv.at[h], {"blk": p})

    pl.semaphore_wait(barrier, len(near) + len(beside))
    for r, ring in enumerate(rings):
        if r:
            pl.semaphore_wait(near_sem.at[r - 1], len(near))
        if r < len(rings) - 1:
            tell(near_sem.at[r], near)
        for peer in ring:
            send_modes(0, peer)
    loads[0].wait()
    for _, _, p in peers:
        remote(eig_in, eig.at[b], e_send, e_recv, {"blk": p})
    eig[b] = eig_in[...]
    for h in range(2):
        pltpu.make_async_copy(modes.at[0, :, layer_of(z, c, h)], land.at[h, my_rows], in_recv.at[h]).start()
    for peer in peers:
        send_modes(1, peer)

    loads[1].wait()
    loads[2].wait()

    def mass_step(i, acc):
        f = own[:, i].astype(F32)
        w = (dens[i][None] * f).astype(BF16).astype(F32)
        return acc + w * f

    acc = lax.fori_loop(0, layers, mass_step, jnp.zeros((rows, cy, cz), F32))
    mass = jnp.sum(jnp.sum(acc, axis=1), axis=1, keepdims=True)
    lane = lax.broadcasted_iota(jnp.int32, (rows, n_modes), 1)
    sub = lax.broadcasted_iota(jnp.int32, (rows, n_modes), 0)
    mine = lane == sub + b * rows
    mass_row = jnp.sum(jnp.where(mine, mass, 0.0), axis=0, keepdims=True)
    msend[...] = mass_row
    for n, (_, _, p) in enumerate(peers):
        remote(msend, mland.at[n], m_send, m_recv, {"blk": p})
    loads[3].wait()
    drain(coef, load_sem.at[4])
    rounds = leaves // 2 + dofs // 2 - 1
    for r in range(rounds):
        tell(plane_sem.at[r], beside)
        pl.semaphore_wait(plane_sem.at[r], len(beside))

    last_lane = lax.broadcasted_iota(jnp.int32, (n_modes, cz), 1) == cz - 1

    def relayout(h):
        wide[...] = land[h].reshape(n_modes * cy, cz).astype(F32)
        for j in range(cy):
            phi[h, :, j * cz : (j + 1) * cz] = wide[pl.ds(j, n_modes, stride=cy), :].astype(BF16)

    def send_edge(h, send, device):
        part = phi.at[h, :, pl.ds(pl.multiple_of(c * half * cz, half * cz), half * cz)]
        remote(part, edge.at[h], send, h_recv.at[h], device)

    def expand(h):
        e = eig[...].astype(F32).reshape(n_modes, n_modes).astype(BF16)
        for j in range(0, cy, 2):
            v = jnp.dot(e, phi[h, :, j * cz : (j + 2) * cz], preferred_element_type=F32)
            tall[pl.ds(j, n_modes, stride=cy), :] = v[:, :cz]
            tall[pl.ds(j + 1, n_modes, stride=cy), :] = v[:, cz:]
        vecs[h] = tall[...].astype(BF16).reshape(n_modes, cy, cz)
        pltpu.make_async_copy(vecs.at[h, my_rows], vec_out.at[:, layer_of(z, c, h)], out_recv).start()

    def send_vectors(h, some):
        for _, _, p in some:
            block = vecs.at[h, pl.ds(pl.multiple_of(p * rows, rows), rows)]
            remote(block, vec_out.at[:, layer_of(z, c, h)], out_send, out_recv, {"blk": p})

    def images(h, other):
        nxt = wide[pl.ds(0, n_modes, stride=cy), :]
        for j in range(cy):
            f = nxt
            s = coef[h, j : j + 1, :] + 6.0
            side = jnp.where(last_lane, 0.0, pltpu.roll(f, cz - 1, 1))
            if j + 1 < cy:
                nxt = wide[pl.ds(j + 1, n_modes, stride=cy), :]
                side = side + nxt
            if other is not None:
                side = side + phi[other, :, j * cz : (j + 1) * cz].astype(F32)
            lhs[:, j * cz : (j + 1) * cz] = (s * f - 2.0 * side).astype(BF16)
        return lax.dot_general(lhs[...], phi[h], (((1,), (1,)), ((), ())), preferred_element_type=F32)

    def edge_product(h):
        part = phi[h, :, pl.ds(pl.multiple_of((1 - c) * half * cz, half * cz), half * cz)]
        return lax.dot_general(edge[h], part, (((1,), (1,)), ((), ())), preferred_element_type=F32)

    out_order = peers[::-1]
    drain(land.at[0], in_recv.at[0])
    relayout(0)
    send_edge(0, h0_send, {"dof": py, "blk": pb})
    drain(eig.at[pl.ds(0, blks - 1)], e_recv)
    expand(0)
    send_vectors(0, out_order[:first_part])
    kfull[...] = images(0, None)

    drain(land.at[1], in_recv.at[1])
    relayout(1)
    send_edge(1, h1_send, {"blk": z * 2 + (1 - c)})
    kfull[...] += images(1, 0)
    drain(edge.at[0], h_recv.at[0])
    kfull[...] += edge_weight * edge_product(0)
    drain(edge.at[1], h_recv.at[1])
    total = kfull[...] - 2.0 * edge_product(1)
    kfull[...] = 0.5 * (total + total.T)
    for i in range(blks):
        ksend[i] = kfull[i * rows : (i + 1) * rows, :].astype(BF16)
    for n, (_, _, p) in enumerate(peers):
        remote(ksend.at[p], kland.at[n], k_send, k_recv, {"blk": p})
    send_vectors(0, out_order[first_part:])
    expand(1)
    send_vectors(1, out_order)

    drain(mland, m_recv)
    mass_total = mass_row
    for n in range(blks - 1):
        mass_total = mass_total + mland[n]
    drain(kland, k_recv)
    k_total = ksend[b].astype(F32)
    for n in range(blks - 1):
        k_total = k_total + kland[n].astype(F32)
    psend[:rows] = k_total
    psend[rows:] = jnp.broadcast_to(mass_total, (rows, n_modes))
    slot = x * dofs + y
    for i, j in plane:
        remote(psend, pland.at[slot], p_send, p_recv, {"leaf": i, "dof": j})
    pland[slot] = psend[...]
    drain(pland.at[pl.ds(0, leaves * dofs - 1)], p_recv)

    per_leaf = []
    for i in range(leaves):
        t = pland[i * dofs]
        for j in range(1, dofs):
            t = t + pland[i * dofs + j]
        per_leaf.append(t)
    root = jnp.zeros((rows, n_modes), F32)
    for i_node in range(node.shape[0]):
        t = jnp.zeros((2 * rows, n_modes), F32)
        for i in range(leaves):
            t = t + jnp.where(parent[i] == i_node, 1.0, 0.0).astype(F32) * per_leaf[i]
        node[i_node] = t[:rows]
        scale = 1.0 / jnp.sqrt(t[rows:])
        scale_own = jnp.sum(jnp.where(mine, scale, 0.0), axis=1, keepdims=True)
        root = root + scale_own * t[:rows] * scale
    root_sum[...] = root
    results = [
        pltpu.make_async_copy(node, node_out, load_sem.at[5]),
        pltpu.make_async_copy(root_sum, root_out, load_sem.at[6]),
    ]
    for cp in results:
        cp.start()

    drain(modes.at[0, :, pl.ds(0, 2 * blks - 2)], in_send)
    drain(eig.at[pl.ds(0, blks - 1)], e_send)
    drain(kland, k_send)
    drain(mland, m_send)
    drain(pland.at[pl.ds(0, leaves * dofs - 1)], p_send)
    drain(edge.at[0], h0_send)
    drain(edge.at[1], h1_send)
    for cp in results:
        cp.wait()
    drain(modes.at[0, :, pl.ds(0, 2 * blks - 2)], out_send)
    drain(vec_out, out_recv)


def finish(*refs):
    count = len(refs) // 2
    sem = refs[-1]
    cps = [pltpu.make_async_copy(refs[i], refs[count + i], sem.at[i]) for i in range(count)]
    for cp in cps:
        cp.start()
    for cp in cps:
        cp.wait()


def solution(mesh):
    leaves, dofs, blks = (mesh.shape[a] for a in ("leaf", "dof", "blk"))

    def body(modes, stiffness, density, eigen_blocks, parent):
        _, rows, layers, cy, cz = modes.shape
        n_modes = rows * blks
        cells = cy * cz
        others = blks - 1
        dma = pltpu.SemaphoreType.DMA
        any_spec = pl.BlockSpec(memory_space=pl.ANY)
        vmem_spec = pl.BlockSpec(memory_space=pltpu.VMEM)
        shapes = (
            jax.ShapeDtypeStruct((leaves // 2, rows, n_modes), F32),
            jax.ShapeDtypeStruct((rows, n_modes), F32),
            jax.ShapeDtypeStruct((rows, layers, cy, cz), BF16),
        )
        results = pl.pallas_call(
            lambda *refs: kernel((leaves, dofs, blks), FIRST_PART, *refs),
            out_shape=tuple(pltpu.VMEM(s.shape, s.dtype) for s in shapes),
            in_specs=[any_spec] * 5,
            out_specs=(any_spec,) * 3,
            scratch_shapes=[
                pltpu.SMEM((leaves,), jnp.int32),
                pltpu.VMEM((leaves // 2, rows, n_modes), F32),
                pltpu.VMEM((rows, n_modes), F32),
                pltpu.VMEM((rows, layers, cy, cz), BF16),
                pltpu.VMEM((layers, cy, cz), F32),
                pltpu.VMEM((2, cy, cz), F32),
                pltpu.VMEM((rows, n_modes), BF16),
                pltpu.VMEM((blks, rows, n_modes), BF16),
                pltpu.VMEM((2, n_modes, cy, cz), BF16),
                pltpu.VMEM((n_modes * cy, cz), F32),
                pltpu.VMEM((2, n_modes, cells), BF16),
                pltpu.VMEM((n_modes, cells), BF16),
                pltpu.VMEM((n_modes * cy, cz), F32),
                pltpu.VMEM((2, n_modes, cy, cz), BF16),
                pltpu.VMEM((2, n_modes, cells // 2), BF16),
                pltpu.VMEM((n_modes, n_modes), F32),
                pltpu.VMEM((blks, rows, n_modes), BF16),
                pltpu.VMEM((others, rows, n_modes), BF16),
                pltpu.VMEM((1, n_modes), F32),
                pltpu.VMEM((others, 1, n_modes), F32),
                pltpu.VMEM((2 * rows, n_modes), F32),
                pltpu.VMEM((leaves * dofs, 2 * rows, n_modes), F32),
                dma((7,)),
                dma((2,)),
                dma(()),
                dma((2,)),
                dma((4,)),
                dma((8,)),
                pltpu.SemaphoreType.REGULAR((blks // 4,)),
                pltpu.SemaphoreType.REGULAR((leaves // 2 + dofs // 2 - 1,)),
            ],
            compiler_params=pltpu.CompilerParams(
                collective_id=0, has_side_effects=True
            ),
            name="tree",
        )(modes, stiffness, density, jnp.swapaxes(eigen_blocks, 1, 2), parent)
        node, root, vectors = pl.pallas_call(
            finish,
            out_shape=shapes,
            in_specs=[vmem_spec] * 3,
            out_specs=(any_spec,) * 3,
            scratch_shapes=[dma((3,))],
            compiler_params=pltpu.CompilerParams(vmem_limit_bytes=4 << 20),
            name="finish",
        )(*results)
        return node, root, vectors[None]

    in_specs = (
        P("leaf", "blk", "dof", None, None),
        P("leaf", "dof", None, None),
        P("leaf", "dof", None, None),
        P("leaf", None, "blk"),
        P(),
    )
    out_specs = (P(None, "blk", None), P("blk", None), P("leaf", "blk", "dof", None, None))
    return jax.shard_map(body, mesh=mesh, in_specs=in_specs, out_specs=out_specs, check_vma=False)
```

time: 72.9 us -> 62.5 us (0.86)
  local copies, waits for them, and re-layouts: 5.67 us -> 0 us
  Pallas kernels: 66.4 us -> 61.8 us
    unnamed x6 -> x0, local copies, waits for them, and re-layouts: 5.67 us -> none
    pallas_call x1 -> x2, Pallas kernels: 66.4 us -> 61.8 us  [the longest x1 60.8 us: body(): pl.pallas_call(lambda *refs: kernel((leaves, dofs, blks), FIRST_PART, *re...]
where the time goes in v2:
time: 62.5 us; the launch traced here: 62.4 us
  Pallas kernels  61.8 us (99%)
  between operations  0.64 us (1%)
    pallas_call x1, Pallas kernels, body(): pl.pallas_call(lambda *refs: kernel((leaves, dofs, blks), FIRST_PART, *re...  60.8 us

profile of v2, /device:TPU:1, one launch (start us, length us, event | category | flops | bytes accessed | tf_op | source)
XLA Modules:
  0.0 62.4 jit_solution(16400116423492070600)
XLA Ops:
  0.6 60.8 %tree.1 = (f32[2,8,128]{2,1,0:T(8,128)S(1)}, f32[8,128]{1,0:T(8,128)S(1)}, bf16[8,32,16,128]{3,2,1,0:T(8,128)(2,1)S(1)}) custom-call(bf16[1,8,32,16,128]{4,3,2,1,0:T(8,128)(2,1)} %refs_0_.1, f32[1,32,16,128]{3,2,1,0:T(8,128)} %refs_1_.1, f32[1,32,16,128]{3,2,1,0:T(8,128)} %refs_2_.1, bf16[1,8,128]{2,1,0:T(8,128)(2,1)} %bitcast.2, s32[4]{0:T(128)} %refs_4_.1), custom_call_target="tpu_custom_call" | custom-call | tf_op jit(solution)/shard_map/tree/pallas_call | solution.py:321
  61.4 1.0 %finish.1 = (f32[2,8,128]{2,1,0:T(8,128)}, f32[8,128]{1,0:T(8,128)}, bf16[8,32,16,128]{3,2,1,0:T(8,128)(2,1)}) custom-call(f32[2,8,128]{2,1,0:T(8,128)S(1)} %get-tuple-element.9.refs_0_, f32[8,128]{1,0:T(8,128)S(1)} %get-tuple-element.10.refs_1_, bf16[8,32,16,128]{3,2,1,0:T(8,128)(2,1)S(1)} %get-tuple-element.11.refs_2_), custom_call_target="tpu_custom_call" | custom-call | tf_op jit(solution)/shard_map/finish/pallas_call | solution.py:363

commit v3 on v2

--- a/solution.py
+++ b/solution.py
@@ -8,7 +8,8 @@
 MESH = pl.DeviceIdType.MESH
 F32 = jnp.float32
 BF16 = jnp.bfloat16
-FIRST_PART = 8
+FIRST_PART = 9
+IN_PART = 12
 
 
 def ring_peers(chips):
@@ -41,7 +42,6 @@
     own,
     dens,
     coef,
-    eig_in,
     eig,
     land,
     wide,
@@ -73,8 +73,8 @@
     half = cy // 2
     x, y, b = lax.axis_index("leaf"), lax.axis_index("dof"), lax.axis_index("blk")
     z, c = b // 2, lax.rem(b, 2)
-    e_recv, k_recv, m_recv, p_recv = (small_recv.at[i] for i in range(4))
-    in_send, e_send, out_send, k_send, m_send, p_send, h0_send, h1_send = (send_sem.at[i] for i in range(8))
+    e_recv, k_recv, m_recv, p_recv, f_recv = (small_recv.at[i] for i in range(5))
+    in_send, e_send, out_send, k_send, m_send, p_send, h0_send, h1_send, f_send = (send_sem.at[i] for i in range(9))
     my_rows = pl.ds(pl.multiple_of(b * rows, rows), rows)
 
     def layer_of(zz, cc, h):
@@ -82,7 +82,7 @@
 
     def column_peer(dz, dc):
         zz = lax.rem(z + dz, chips)
-        cc = lax.rem(c + dc, 2)
+        cc = 1 - c if dc else c
         return zz, cc, zz * 2 + cc
 
     rings = [[column_peer(dz, dc) for dz, dc in ring] for ring in ring_peers(chips)]
@@ -96,7 +96,6 @@
     py = lax.rem(y + step * wraps + dofs, dofs)
     pb = pz * 2 + (1 - c)
     at_end = jnp.where(c == 1, jnp.where(y == dofs - 1, 1, 0), jnp.where(y == 0, 1, 0)) * wraps
-    edge_weight = jnp.where(at_end == 1, 0.0, -2.0).astype(F32)
 
     near = [{"blk": p} for _, _, p in rings[0]]
     beside = [
@@ -110,15 +109,33 @@
         for device in devices:
             pl.semaphore_signal(sem, inc=1, device_id=device, device_id_type=MESH)
 
+    def ahead(sem, up):
+        for axis, i, n in (("leaf", x, leaves), ("dof", y, dofs)):
+            step, first, last = (1, 0, n - 1) if up else (-1, n - 1, 0)
+
+            @pl.when(i != last)
+            def _():
+                tell(sem, [{axis: i + step}])
+
+            @pl.when(i == first)
+            def _():
+                tell(sem, [{axis: last}])
+
+    def one(condition):
+        return jnp.where(condition, 1, 0)
+
+    heard_up = one(x > 0) + one(x == leaves - 1) + one(y > 0) + one(y == dofs - 1)
+    heard_down = 2 * 2 - heard_up
+
     barrier = pltpu.get_barrier_semaphore()
-    tell(barrier, near + beside)
+    tell(barrier, near)
+    ahead(barrier, True)
     loads = [
-        pltpu.make_async_copy(eigen.at[0], eig_in, load_sem.at[0]),
-        pltpu.make_async_copy(modes.at[0], own, load_sem.at[1]),
-        pltpu.make_async_copy(density.at[0], dens, load_sem.at[2]),
-        pltpu.make_async_copy(parent_in, parent, load_sem.at[3]),
-        pltpu.make_async_copy(stiffness.at[0, pl.ds(layer_of(z, c, 0), 1)], coef.at[pl.ds(0, 1)], load_sem.at[4]),
-        pltpu.make_async_copy(stiffness.at[0, pl.ds(layer_of(z, c, 1), 1)], coef.at[pl.ds(1, 1)], load_sem.at[4]),
+        pltpu.make_async_copy(modes.at[0], own, load_sem.at[0]),
+        pltpu.make_async_copy(density.at[0], dens, load_sem.at[1]),
+        pltpu.make_async_copy(parent_in, parent, load_sem.at[2]),
+        pltpu.make_async_copy(stiffness.at[0, pl.ds(layer_of(z, c, 0), 1)], coef.at[pl.ds(0, 1)], load_sem.at[3]),
+        pltpu.make_async_copy(stiffness.at[0, pl.ds(layer_of(z, c, 1), 1)], coef.at[pl.ds(1, 1)], load_sem.at[3]),
     ]
     for cp in loads:
         cp.start()
@@ -130,25 +147,33 @@
         zz, cc, p = peer
         remote(modes.at[0, :, layer_of(zz, cc, h)], land.at[h, my_rows], in_send, in_recv.at[h], {"blk": p})
 
-    pl.semaphore_wait(barrier, len(near) + len(beside))
+    pl.semaphore_wait(barrier, heard_up + len(near))
+    early, late = [], []
     for r, ring in enumerate(rings):
         if r:
             pl.semaphore_wait(near_sem.at[r - 1], len(near))
         if r < len(rings) - 1:
             tell(near_sem.at[r], near)
+        if r == 0:
+            ahead(plane_sem.at[0], False)
         for peer in ring:
             send_modes(0, peer)
-    loads[0].wait()
-    for _, _, p in peers:
-        remote(eig_in, eig.at[b], e_send, e_recv, {"blk": p})
-    eig[b] = eig_in[...]
+            if r == 0:
+                send_modes(1, peer)
+                early.append(peer)
+            else:
+                late.insert(0, peer)
+        for zz, cc, p in ring:
+            if cc is c:
+                remote(eigen.at[0], eig.at[c, z], e_send, e_recv, {"blk": p})
     for h in range(2):
         pltpu.make_async_copy(modes.at[0, :, layer_of(z, c, h)], land.at[h, my_rows], in_recv.at[h]).start()
-    for peer in peers:
+    pltpu.make_async_copy(eigen.at[0], eig.at[c, z], e_recv).start()
+    for peer in late[:IN_PART]:
         send_modes(1, peer)
 
+    loads[0].wait()
     loads[1].wait()
-    loads[2].wait()
 
     def mass_step(i, acc):
         f = own[:, i].astype(F32)
@@ -164,12 +189,18 @@
     msend[...] = mass_row
     for n, (_, _, p) in enumerate(peers):
         remote(msend, mland.at[n], m_send, m_recv, {"blk": p})
-    loads[3].wait()
-    drain(coef, load_sem.at[4])
-    rounds = leaves // 2 + dofs // 2 - 1
-    for r in range(rounds):
+    loads[2].wait()
+    drain(coef, load_sem.at[3])
+    def plane_round(r):
         tell(plane_sem.at[r], beside)
         pl.semaphore_wait(plane_sem.at[r], len(beside))
+
+
+    @pl.when(heard_down > 0)
+    def _():
+        pl.semaphore_wait(plane_sem.at[0], heard_down)
+
+    plane_round(1)
 
     last_lane = lax.broadcasted_iota(jnp.int32, (n_modes, cz), 1) == cz - 1
 
@@ -181,6 +212,9 @@
     def send_edge(h, send, device):
         part = phi.at[h, :, pl.ds(pl.multiple_of(c * half * cz, half * cz), half * cz)]
         remote(part, edge.at[h], send, h_recv.at[h], device)
+
+    def block_of(zz, cc):
+        return pl.ds(pl.multiple_of((cc * chips + zz) * rows, rows), rows)
 
     def expand(h):
         e = eig[...].astype(F32).reshape(n_modes, n_modes).astype(BF16)
@@ -189,12 +223,11 @@
             tall[pl.ds(j, n_modes, stride=cy), :] = v[:, :cz]
             tall[pl.ds(j + 1, n_modes, stride=cy), :] = v[:, cz:]
         vecs[h] = tall[...].astype(BF16).reshape(n_modes, cy, cz)
-        pltpu.make_async_copy(vecs.at[h, my_rows], vec_out.at[:, layer_of(z, c, h)], out_recv).start()
+        pltpu.make_async_copy(vecs.at[h, block_of(z, c)], vec_out.at[:, layer_of(z, c, h)], out_recv).start()
 
     def send_vectors(h, some):
-        for _, _, p in some:
-            block = vecs.at[h, pl.ds(pl.multiple_of(p * rows, rows), rows)]
-            remote(block, vec_out.at[:, layer_of(z, c, h)], out_send, out_recv, {"blk": p})
+        for zz, cc, p in some:
+            remote(vecs.at[h, block_of(zz, cc)], vec_out.at[:, layer_of(z, c, h)], out_send, out_recv, {"blk": p})
 
     def images(h, other):
         nxt = wide[pl.ds(0, n_modes, stride=cy), :]
@@ -217,18 +250,32 @@
     out_order = peers[::-1]
     drain(land.at[0], in_recv.at[0])
     relayout(0)
-    send_edge(0, h0_send, {"dof": py, "blk": pb})
-    drain(eig.at[pl.ds(0, blks - 1)], e_recv)
+
+    @pl.when(at_end == 0)
+    def _():
+        send_edge(0, h0_send, {"dof": py, "blk": pb})
+
+    for peer in late[IN_PART:]:
+        send_modes(1, peer)
+    drain(eig.at[0], e_recv)
+    remote(eig.at[c], eig.at[c], f_send, f_recv, {"blk": z * 2 + (1 - c)})
+    kfull[...] = images(0, None)
+    drain(eig.at[0], f_recv)
     expand(0)
     send_vectors(0, out_order[:first_part])
-    kfull[...] = images(0, None)
+    for r in range(2, leaves // 2 + dofs // 2):
+        plane_round(r)
 
     drain(land.at[1], in_recv.at[1])
     relayout(1)
     send_edge(1, h1_send, {"blk": z * 2 + (1 - c)})
     kfull[...] += images(1, 0)
-    drain(edge.at[0], h_recv.at[0])
-    kfull[...] += edge_weight * edge_product(0)
+
+    @pl.when(at_end == 0)
+    def _():
+        drain(edge.at[0], h_recv.at[0])
+        kfull[...] -= 2.0 * edge_product(0)
+
     drain(edge.at[1], h_recv.at[1])
     total = kfull[...] - 2.0 * edge_product(1)
     kfull[...] = 0.5 * (total + total.T)
@@ -273,18 +320,23 @@
         root = root + scale_own * t[:rows] * scale
     root_sum[...] = root
     results = [
-        pltpu.make_async_copy(node, node_out, load_sem.at[5]),
-        pltpu.make_async_copy(root_sum, root_out, load_sem.at[6]),
+        pltpu.make_async_copy(node, node_out, load_sem.at[4]),
+        pltpu.make_async_copy(root_sum, root_out, load_sem.at[5]),
     ]
     for cp in results:
         cp.start()
 
     drain(modes.at[0, :, pl.ds(0, 2 * blks - 2)], in_send)
-    drain(eig.at[pl.ds(0, blks - 1)], e_send)
+    drain(eig.at[0, pl.ds(0, chips - 1)], e_send)
+    drain(eig.at[0], f_send)
     drain(kland, k_send)
     drain(mland, m_send)
     drain(pland.at[pl.ds(0, leaves * dofs - 1)], p_send)
-    drain(edge.at[0], h0_send)
+
+    @pl.when(at_end == 0)
+    def _():
+        drain(edge.at[0], h0_send)
+
     drain(edge.at[1], h1_send)
     for cp in results:
         cp.wait()
@@ -330,8 +382,7 @@
                 pltpu.VMEM((rows, layers, cy, cz), BF16),
                 pltpu.VMEM((layers, cy, cz), F32),
                 pltpu.VMEM((2, cy, cz), F32),
-                pltpu.VMEM((rows, n_modes), BF16),
-                pltpu.VMEM((blks, rows, n_modes), BF16),
+                pltpu.VMEM((2, blks // 2, rows, n_modes), BF16),
                 pltpu.VMEM((2, n_modes, cy, cz), BF16),
                 pltpu.VMEM((n_modes * cy, cz), F32),
                 pltpu.VMEM((2, n_modes, cells), BF16),
@@ -346,14 +397,14 @@
                 pltpu.VMEM((others, 1, n_modes), F32),
                 pltpu.VMEM((2 * rows, n_modes), F32),
                 pltpu.VMEM((leaves * dofs, 2 * rows, n_modes), F32),
-                dma((7,)),
+                dma((6,)),
                 dma((2,)),
                 dma(()),
                 dma((2,)),
-                dma((4,)),
-                dma((8,)),
+                dma((5,)),
+                dma((9,)),
                 pltpu.SemaphoreType.REGULAR((blks // 4,)),
-                pltpu.SemaphoreType.REGULAR((leaves // 2 + dofs // 2 - 1,)),
+                pltpu.SemaphoreType.REGULAR((leaves // 2 + dofs // 2,)),
             ],
             compiler_params=pltpu.CompilerParams(
                 collective_id=0, has_side_effects=True

time: 62.5 us -> 60.1 us (0.962)
  Pallas kernels: 61.8 us -> 59.4 us
    pallas_call x1, Pallas kernels: 60.8 us -> 58.4 us  [body(): pl.pallas_call(lambda *refs: kernel((leaves, dofs, blks), FIRST_PART, *re...]
where the time goes in v3:
time: 60.1 us; the launch traced here: 60 us
  Pallas kernels  59.4 us (99%)
  between operations  0.64 us (1%)
    pallas_call x1, Pallas kernels, body(): pl.pallas_call(lambda *refs: kernel((leaves, dofs, blks), FIRST_PART, *re...  58.4 us

profile of v3, /device:TPU:1, one launch (start us, length us, event | category | flops | bytes accessed | tf_op | source)
XLA Modules:
  0.0 60.0 jit_solution(15574354842947910433)
XLA Ops:
  0.6 58.4 %tree.1 = (f32[2,8,128]{2,1,0:T(8,128)S(1)}, f32[8,128]{1,0:T(8,128)S(1)}, bf16[8,32,16,128]{3,2,1,0:T(8,128)(2,1)S(1)}) custom-call(bf16[1,8,32,16,128]{4,3,2,1,0:T(8,128)(2,1)} %refs_0_.1, f32[1,32,16,128]{3,2,1,0:T(8,128)} %refs_1_.1, f32[1,32,16,128]{3,2,1,0:T(8,128)} %refs_2_.1, bf16[1,8,128]{2,1,0:T(8,128)(2,1)} %bitcast.2, s32[4]{0:T(128)} %refs_4_.1), custom_call_target="tpu_custom_call" | custom-call | tf_op jit(solution)/shard_map/tree/pallas_call | solution.py:373
  59.0 1.0 %finish.1 = (f32[2,8,128]{2,1,0:T(8,128)}, f32[8,128]{1,0:T(8,128)}, bf16[8,32,16,128]{3,2,1,0:T(8,128)(2,1)}) custom-call(f32[2,8,128]{2,1,0:T(8,128)S(1)} %get-tuple-element.9.refs_0_, f32[8,128]{1,0:T(8,128)S(1)} %get-tuple-element.10.refs_1_, bf16[8,32,16,128]{3,2,1,0:T(8,128)(2,1)S(1)} %get-tuple-element.11.refs_2_), custom_call_target="tpu_custom_call" | custom-call | tf_op jit(solution)/shard_map/finish/pallas_call | solution.py:414

commit v4 on v3

--- a/solution.py
+++ b/solution.py
@@ -8,7 +8,7 @@
 MESH = pl.DeviceIdType.MESH
 F32 = jnp.float32
 BF16 = jnp.bfloat16
-FIRST_PART = 9
+FIRST_PART = 8
 IN_PART = 12
 
 
@@ -225,9 +225,30 @@
         vecs[h] = tall[...].astype(BF16).reshape(n_modes, cy, cz)
         pltpu.make_async_copy(vecs.at[h, block_of(z, c)], vec_out.at[:, layer_of(z, c, h)], out_recv).start()
 
-    def send_vectors(h, some):
-        for zz, cc, p in some:
-            remote(vecs.at[h, block_of(zz, cc)], vec_out.at[:, layer_of(z, c, h)], out_send, out_recv, {"blk": p})
+    def send_block(h, zz, cc):
+        remote(vecs.at[h, block_of(zz, cc)], vec_out.at[:, layer_of(z, c, h)], out_send, out_recv, {"blk": zz * 2 + cc})
+
+    def send_vectors(h, some, first=()):
+        for place, (zz, cc, p) in enumerate(some):
+            for at, chip in first:
+                if at == place:
+
+                    @pl.when(z != chip)
+                    def _():
+                        for core in range(2):
+                            send_block(h, chip, core)
+
+            if first:
+                others = zz == zz
+                for _, chip in first:
+                    others = others & (zz != chip)
+
+                @pl.when(others | (zz == z))
+                def _():
+                    send_block(h, zz, cc)
+
+            else:
+                send_block(h, zz, cc)
 
     def images(h, other):
         nxt = wide[pl.ds(0, n_modes, stride=cy), :]
@@ -270,6 +291,7 @@
     relayout(1)
     send_edge(1, h1_send, {"blk": z * 2 + (1 - c)})
     kfull[...] += images(1, 0)
+    expand(1)
 
     @pl.when(at_end == 0)
     def _():
@@ -281,11 +303,10 @@
     kfull[...] = 0.5 * (total + total.T)
     for i in range(blks):
         ksend[i] = kfull[i * rows : (i + 1) * rows, :].astype(BF16)
-    for n, (_, _, p) in enumerate(peers):
+    for n, (_, _, p) in reversed(list(enumerate(peers))):
         remote(ksend.at[p], kland.at[n], k_send, k_recv, {"blk": p})
     send_vectors(0, out_order[first_part:])
-    expand(1)
-    send_vectors(1, out_order)
+    send_vectors(1, out_order, ((0, 0), (4, 1)))
 
     drain(mland, m_recv)
     mass_total = mass_row

time: 60.1 us -> 58.5 us (0.973); the launches traced: 60 us -> 57.8 us
  Pallas kernels: 59.4 us -> 57.2 us
    pallas_call x1, Pallas kernels: 58.4 us -> 56.2 us  [body(): pl.pallas_call(lambda *refs: kernel((leaves, dofs, blks), FIRST_PART, *re...]
where the time goes in v4:
time: 58.5 us; the launch traced here: 57.8 us
  Pallas kernels  57.2 us (98%)
  between operations  0.64 us (1%)
    pallas_call x1, Pallas kernels, body(): pl.pallas_call(lambda *refs: kernel((leaves, dofs, blks), FIRST_PART, *re...  56.2 us

profile of v4, /device:TPU:1, one launch (start us, length us, event | category | flops | bytes accessed | tf_op | source)
XLA Modules:
  0.0 57.8 jit_solution(6595730538793879014)
XLA Ops:
  0.6 56.2 %tree.1 = (f32[2,8,128]{2,1,0:T(8,128)S(1)}, f32[8,128]{1,0:T(8,128)S(1)}, bf16[8,32,16,128]{3,2,1,0:T(8,128)(2,1)S(1)}) custom-call(bf16[1,8,32,16,128]{4,3,2,1,0:T(8,128)(2,1)} %refs_0_.1, f32[1,32,16,128]{3,2,1,0:T(8,128)} %refs_1_.1, f32[1,32,16,128]{3,2,1,0:T(8,128)} %refs_2_.1, bf16[1,8,128]{2,1,0:T(8,128)(2,1)} %bitcast.2, s32[4]{0:T(128)} %refs_4_.1), custom_call_target="tpu_custom_call" | custom-call | tf_op jit(solution)/shard_map/tree/pallas_call | solution.py:394
  56.8 1.0 %finish.1 = (f32[2,8,128]{2,1,0:T(8,128)}, f32[8,128]{1,0:T(8,128)}, bf16[8,32,16,128]{3,2,1,0:T(8,128)(2,1)}) custom-call(f32[2,8,128]{2,1,0:T(8,128)S(1)} %get-tuple-element.9.refs_0_, f32[8,128]{1,0:T(8,128)S(1)} %get-tuple-element.10.refs_1_, bf16[8,32,16,128]{3,2,1,0:T(8,128)(2,1)S(1)} %get-tuple-element.11.refs_2_), custom_call_target="tpu_custom_call" | custom-call | tf_op jit(solution)/shard_map/finish/pallas_call | solution.py:435

commit v5 on v4

--- a/solution.py
+++ b/solution.py
@@ -51,6 +51,8 @@
     vecs,
     edge,
     kfull,
+    pair_out,
+    pair_in,
     ksend,
     kland,
     msend,
@@ -73,8 +75,10 @@
     half = cy // 2
     x, y, b = lax.axis_index("leaf"), lax.axis_index("dof"), lax.axis_index("blk")
     z, c = b // 2, lax.rem(b, 2)
-    e_recv, k_recv, m_recv, p_recv, f_recv = (small_recv.at[i] for i in range(5))
-    in_send, e_send, out_send, k_send, m_send, p_send, h0_send, h1_send, f_send = (send_sem.at[i] for i in range(9))
+    e_recv, k_recv, m_recv, p_recv, f_recv, pair_recv = (small_recv.at[i] for i in range(6))
+    in_send, e_send, out_send, k_send, m_send, p_send, h0_send, h1_send, f_send, pair_send = (
+        send_sem.at[i] for i in range(10)
+    )
     my_rows = pl.ds(pl.multiple_of(b * rows, rows), rows)
 
     def layer_of(zz, cc, h):
@@ -186,9 +190,6 @@
     sub = lax.broadcasted_iota(jnp.int32, (rows, n_modes), 0)
     mine = lane == sub + b * rows
     mass_row = jnp.sum(jnp.where(mine, mass, 0.0), axis=0, keepdims=True)
-    msend[...] = mass_row
-    for n, (_, _, p) in enumerate(peers):
-        remote(msend, mland.at[n], m_send, m_recv, {"blk": p})
     loads[2].wait()
     drain(coef, load_sem.at[3])
     def plane_round(r):
@@ -269,6 +270,17 @@
         return lax.dot_general(edge[h], part, (((1,), (1,)), ((), ())), preferred_element_type=F32)
 
     out_order = peers[::-1]
+
+    def toward(k, dc, sign):
+        zz = lax.rem(z + sign * step * k + chips, chips)
+        cc = 1 - c if dc else c
+        return zz, cc, zz * 2 + cc
+
+    away = [toward(k, dc, -1) for k in range(chips // 2 - 1, 0, -1) for dc in (1, 0)]
+    along = [toward(k, dc, 1) for k in range(chips // 2 - 1, 0, -1) for dc in (1, 0)]
+    across = [toward(chips // 2, dc, 1) for dc in (1, 0)]
+    sibling = [column_peer(0, 1)]
+    out0_order = across + along + away + sibling
     drain(land.at[0], in_recv.at[0])
     relayout(0)
 
@@ -283,7 +295,7 @@
     kfull[...] = images(0, None)
     drain(eig.at[0], f_recv)
     expand(0)
-    send_vectors(0, out_order[:first_part])
+    send_vectors(0, out0_order[:first_part])
     for r in range(2, leaves // 2 + dofs // 2):
         plane_round(r)
 
@@ -301,20 +313,33 @@
     drain(edge.at[1], h_recv.at[1])
     total = kfull[...] - 2.0 * edge_product(1)
     kfull[...] = 0.5 * (total + total.T)
-    for i in range(blks):
-        ksend[i] = kfull[i * rows : (i + 1) * rows, :].astype(BF16)
-    for n, (_, _, p) in reversed(list(enumerate(peers))):
-        remote(ksend.at[p], kland.at[n], k_send, k_recv, {"blk": p})
-    send_vectors(0, out_order[first_part:])
-    send_vectors(1, out_order, ((0, 0), (4, 1)))
+
+    def block_rows(zz, cc):
+        return pl.ds(pl.multiple_of((zz * 2 + cc) * rows, rows), rows)
+
+    for zz in range(chips):
+        pair_out[zz] = kfull[block_rows(zz, 1 - c), :]
+    pair_out[chips] = jnp.broadcast_to(mass_row, (rows, n_modes))
+    remote(pair_out, pair_in, pair_send, pair_recv, {"blk": z * 2 + (1 - c)})
+    drain(pair_in, pair_recv)
+    for zz in range(chips):
+        ksend[zz] = (kfull[block_rows(zz, c), :] + pair_in[zz]).astype(BF16)
+    mass_pair = mass_row + pair_in[chips][:1]
+    msend[...] = mass_pair
+    same_core = [(zz, p) for zz, cc, p in peers[::-1] if cc is c]
+    for n, (zz, p) in enumerate(same_core):
+        remote(ksend.at[zz], kland.at[n], k_send, k_recv, {"blk": p})
+        remote(msend, mland.at[n], m_send, m_recv, {"blk": p})
+    send_vectors(0, out0_order[first_part:])
+    send_vectors(1, out_order, ((0, 0), (3, 1), (7, 2)))
 
     drain(mland, m_recv)
-    mass_total = mass_row
-    for n in range(blks - 1):
+    mass_total = mass_pair
+    for n in range(chips - 1):
         mass_total = mass_total + mland[n]
     drain(kland, k_recv)
-    k_total = ksend[b].astype(F32)
-    for n in range(blks - 1):
+    k_total = ksend[z].astype(F32)
+    for n in range(chips - 1):
         k_total = k_total + kland[n].astype(F32)
     psend[:rows] = k_total
     psend[rows:] = jnp.broadcast_to(mass_total, (rows, n_modes))
@@ -351,6 +376,7 @@
     drain(eig.at[0, pl.ds(0, chips - 1)], e_send)
     drain(eig.at[0], f_send)
     drain(kland, k_send)
+    drain(pair_in, pair_send)
     drain(mland, m_send)
     drain(pland.at[pl.ds(0, leaves * dofs - 1)], p_send)
 
@@ -382,7 +408,7 @@
         _, rows, layers, cy, cz = modes.shape
         n_modes = rows * blks
         cells = cy * cz
-        others = blks - 1
+        others = blks // 2 - 1
         dma = pltpu.SemaphoreType.DMA
         any_spec = pl.BlockSpec(memory_space=pl.ANY)
         vmem_spec = pl.BlockSpec(memory_space=pltpu.VMEM)
@@ -412,7 +438,9 @@
                 pltpu.VMEM((2, n_modes, cy, cz), BF16),
                 pltpu.VMEM((2, n_modes, cells // 2), BF16),
                 pltpu.VMEM((n_modes, n_modes), F32),
-                pltpu.VMEM((blks, rows, n_modes), BF16),
+                pltpu.VMEM((blks // 2 + 1, rows, n_modes), F32),
+                pltpu.VMEM((blks // 2 + 1, rows, n_modes), F32),
+                pltpu.VMEM((blks // 2, rows, n_modes), BF16),
                 pltpu.VMEM((others, rows, n_modes), BF16),
                 pltpu.VMEM((1, n_modes), F32),
                 pltpu.VMEM((others, 1, n_modes), F32),
@@ -422,8 +450,8 @@
                 dma((2,)),
                 dma(()),
                 dma((2,)),
-                dma((5,)),
-                dma((9,)),
+                dma((6,)),
+                dma((10,)),
                 pltpu.SemaphoreType.REGULAR((blks // 4,)),
                 pltpu.SemaphoreType.REGULAR((leaves // 2 + dofs // 2,)),
             ],

time: 58.5 us -> 58 us (level)
  Pallas kernels: 57.2 us -> 56.4 us
    pallas_call x1, Pallas kernels: 56.2 us -> 55.4 us  [body(): pl.pallas_call(lambda *refs: kernel((leaves, dofs, blks), FIRST_PART, *re...]
where the time goes in v5:
time: 58 us; the launch traced here: 57.1 us
  Pallas kernels  56.4 us (97%)
  between operations  0.64 us (1%)
    pallas_call x1, Pallas kernels, body(): pl.pallas_call(lambda *refs: kernel((leaves, dofs, blks), FIRST_PART, *re...  55.4 us

profile of v5, /device:TPU:1, one launch (start us, length us, event | category | flops | bytes accessed | tf_op | source)
XLA Modules:
  0.0 57.1 jit_solution(13957841209608668446)
XLA Ops:
  0.6 55.4 %tree.1 = (f32[2,8,128]{2,1,0:T(8,128)S(1)}, f32[8,128]{1,0:T(8,128)S(1)}, bf16[8,32,16,128]{3,2,1,0:T(8,128)(2,1)S(1)}) custom-call(bf16[1,8,32,16,128]{4,3,2,1,0:T(8,128)(2,1)} %refs_0_.1, f32[1,32,16,128]{3,2,1,0:T(8,128)} %refs_1_.1, f32[1,32,16,128]{3,2,1,0:T(8,128)} %refs_2_.1, bf16[1,8,128]{2,1,0:T(8,128)(2,1)} %bitcast.2, s32[4]{0:T(128)} %refs_4_.1), custom_call_target="tpu_custom_call" | custom-call | tf_op jit(solution)/shard_map/tree/pallas_call | solution.py:420
  56.1 1.0 %finish.1 = (f32[2,8,128]{2,1,0:T(8,128)}, f32[8,128]{1,0:T(8,128)}, bf16[8,32,16,128]{3,2,1,0:T(8,128)(2,1)}) custom-call(f32[2,8,128]{2,1,0:T(8,128)S(1)} %get-tuple-element.9.refs_0_, f32[8,128]{1,0:T(8,128)S(1)} %get-tuple-element.10.refs_1_, bf16[8,32,16,128]{3,2,1,0:T(8,128)(2,1)S(1)} %get-tuple-element.11.refs_2_), custom_call_target="tpu_custom_call" | custom-call | tf_op jit(solution)/shard_map/finish/pallas_call | solution.py:463

commit v6 on v5

--- a/solution.py
+++ b/solution.py
@@ -331,7 +331,7 @@
         remote(ksend.at[zz], kland.at[n], k_send, k_recv, {"blk": p})
         remote(msend, mland.at[n], m_send, m_recv, {"blk": p})
     send_vectors(0, out0_order[first_part:])
-    send_vectors(1, out_order, ((0, 0), (3, 1), (7, 2)))
+    send_vectors(1, out_order, ((0, 0), (2, 1), (5, 2), (9, 3)))
 
     drain(mland, m_recv)
     mass_total = mass_pair

time: 58 us -> 58 us (level)
  no operation moved by 1% of the time
where the time goes in v6:
time: 58 us; the launch traced here: 57.5 us
  Pallas kernels  56.9 us (98%)
  between operations  0.64 us (1%)
    pallas_call x1, Pallas kernels, body(): pl.pallas_call(lambda *refs: kernel((leaves, dofs, blks), FIRST_PART, *re...  55.9 us

profile of v6, /device:TPU:1, one launch (start us, length us, event | category | flops | bytes accessed | tf_op | source)
XLA Modules:
  0.0 57.5 jit_solution(17551049439937061636)
XLA Ops:
  0.6 55.9 %tree.1 = (f32[2,8,128]{2,1,0:T(8,128)S(1)}, f32[8,128]{1,0:T(8,128)S(1)}, bf16[8,32,16,128]{3,2,1,0:T(8,128)(2,1)S(1)}) custom-call(bf16[1,8,32,16,128]{4,3,2,1,0:T(8,128)(2,1)} %refs_0_.1, f32[1,32,16,128]{3,2,1,0:T(8,128)} %refs_1_.1, f32[1,32,16,128]{3,2,1,0:T(8,128)} %refs_2_.1, bf16[1,8,128]{2,1,0:T(8,128)(2,1)} %bitcast.2, s32[4]{0:T(128)} %refs_4_.1), custom_call_target="tpu_custom_call" | custom-call | tf_op jit(solution)/shard_map/tree/pallas_call | solution.py:420
  56.5 1.0 %finish.1 = (f32[2,8,128]{2,1,0:T(8,128)}, f32[8,128]{1,0:T(8,128)}, bf16[8,32,16,128]{3,2,1,0:T(8,128)(2,1)}) custom-call(f32[2,8,128]{2,1,0:T(8,128)S(1)} %get-tuple-element.9.refs_0_, f32[8,128]{1,0:T(8,128)S(1)} %get-tuple-element.10.refs_1_, bf16[8,32,16,128]{3,2,1,0:T(8,128)(2,1)S(1)} %get-tuple-element.11.refs_2_), custom_call_target="tpu_custom_call" | custom-call | tf_op jit(solution)/shard_map/finish/pallas_call | solution.py:463
